TPU v7x, 32 devices: a whole 2x2x4 slice. The times are simulated.
32 devices in a mesh: member: 8 (over z, x), dp: 4 (over y, core).
Axes of the slice: x: 2, y: 2, z: 4, core: 2. Of those that a mesh axis runs over, the one named last changes fastest.
Arguments:
- feature_pool: bfloat16 [2048, 256], P('dp'), may hold values from -6 to 6
- labels: int32 [2048], P('dp'), may hold values from 0 to 9
- sample_rows: int32 [1024], P('dp'), may hold values from 0 to 511
- noise_variance: float32 [10], replicated, may hold values from 160 to 640
- first_weight: bfloat16 [16, 256, 2048], P('member', None, 'dp'), may hold values from -6 to 6
- middle_weight: bfloat16 [16, 2048, 2048], P('member', 'dp'), may hold values from -6 to 6
- last_weight: bfloat16 [16, 2048, 10], P('member', 'dp'), may hold values from -6 to 6
Outputs:
- new_first: bfloat16 [16, 256, 2048], P('member', None, 'dp')
- new_middle: bfloat16 [16, 2048, 2048], P('member', 'dp')
- new_last: bfloat16 [16, 2048, 10], P('member', 'dp')
Inputs may be any that keep to these rules, and one draw needn't show every extreme that they name: Sample i reads pool row (i // 256) * 512 + sample_rows[i]. `labels`: class index of each pool row.
All inputs are finite; a program needn't handle non-finite values.
Results may differ from a plain program's by a relative error of at most 0.013.
Values may be sent and summed in bfloat16 or wider, within the bound.
No kernel may reach another device: no remote copies, remote signals or barrier semaphores. Data moves between devices by JAX's collectives and lax.ppermute only.
A program may use at most 128 MiB of HBM per device.

v0:
```python
import jax
import jax.numpy as jnp
from jax import lax
from jax.sharding import PartitionSpec as P

F_IN = 256
H = 2048
precise = lax.Precision.HIGHEST


def update_piece(piece, mixing):
    ensemble = piece.shape[0]
    flat = piece.reshape(ensemble, -1)
    upper = mixing.astype(jnp.bfloat16)
    lower = (mixing - upper.astype(jnp.float32)).astype(jnp.bfloat16)
    stacked = jnp.concatenate([upper.T, lower.T], axis=0)
    both = jnp.dot(stacked, flat, preferred_element_type=jnp.float32)
    product = both[:ensemble] + both[ensemble:]
    column_total = jnp.sum(mixing, axis=0)
    average = jnp.sum(flat, axis=0, dtype=jnp.float32) / ensemble
    renewed = flat.astype(jnp.float32) + product - column_total[:, None] * average[None, :]
    return renewed.astype(jnp.bfloat16).reshape(piece.shape)


def on_device(
    feature_pool, labels, sample_rows, noise_variance, first_weight, middle_weight, last_weight
):
    local_count = sample_rows.shape[0]
    members_here = first_weight.shape[0]
    classes_total = noise_variance.shape[0]
    in_scale = F_IN ** (-0.5)
    hid_scale = H ** (-0.5)
    inputs = feature_pool[sample_rows]
    classes = labels[sample_rows]
    target = (classes[:, None] == jnp.arange(classes_total, dtype=jnp.int32)[None, :]).astype(
        jnp.float32
    )
    first_full, middle_full, last_full = (
        lax.all_gather(first_weight, "dp", axis=2, tiled=True),
        lax.all_gather(middle_weight, "dp", axis=1, tiled=True),
        lax.all_gather(last_weight, "dp", axis=1, tiled=True),
    )
    hidden_one = jnp.tanh(
        jnp.einsum("sf,jfh->jsh", inputs, first_full, preferred_element_type=jnp.float32) * in_scale
    ).astype(jnp.bfloat16)
    hidden_two = jnp.tanh(
        jnp.einsum("jsk,jkh->jsh", hidden_one, middle_full, preferred_element_type=jnp.float32)
        * hid_scale
    ).astype(jnp.bfloat16)
    outputs = (
        jnp.einsum("jsh,jhc->jsc", hidden_two, last_full, preferred_element_type=jnp.float32)
        * hid_scale
    )
    whiten = 1.0 / jnp.sqrt(noise_variance)
    scaled = (outputs * whiten).reshape(members_here, local_count * classes_total)
    observed = (target * whiten).reshape(local_count * classes_total)
    every_member = lax.all_gather(scaled, "member", axis=0, tiled=True)
    center = jnp.mean(every_member, axis=0)
    anomaly = every_member - center
    gram_part = jnp.dot(anomaly, anomaly.T, precision=precise)
    drive_part = jnp.dot(anomaly, observed - center, precision=precise)
    gram_matrix, drive = (
        lax.psum(gram_part.astype(jnp.bfloat16), "dp").astype(jnp.float32),
        lax.psum(drive_part.astype(jnp.bfloat16), "dp").astype(jnp.float32),
    )
    ensemble = gram_matrix.shape[0]
    system = gram_matrix + ensemble * jnp.eye(ensemble, dtype=jnp.float32)
    factor = jnp.linalg.cholesky(system)
    mixing = jax.scipy.linalg.cho_solve((factor, True), drive[:, None] - gram_matrix)
    grouped = (
        lax.all_to_all(first_weight, "member", split_axis=1, concat_axis=0, tiled=True),
        lax.all_to_all(middle_weight, "member", split_axis=1, concat_axis=0, tiled=True),
        lax.all_to_all(last_weight, "member", split_axis=1, concat_axis=0, tiled=True),
    )
    updated = (
        update_piece(grouped[0], mixing),
        update_piece(grouped[1], mixing),
        update_piece(grouped[2], mixing),
    )
    new_first, new_middle, new_last = (
        lax.all_to_all(updated[0], "member", split_axis=0, concat_axis=1, tiled=True),
        lax.all_to_all(updated[1], "member", split_axis=0, concat_axis=1, tiled=True),
        lax.all_to_all(updated[2], "member", split_axis=0, concat_axis=1, tiled=True),
    )
    return (new_first, new_middle, new_last)


def solution(mesh):
    in_specs = (
        P("dp", None),
        P("dp"),
        P("dp"),
        P(),
        P("member", None, "dp"),
        P("member", "dp", None),
        P("member", "dp", None),
    )
    out_specs = (P("member", None, "dp"), P("member", "dp", None), P("member", "dp", None))
    return jax.shard_map(
        on_device, mesh=mesh, in_specs=in_specs, out_specs=out_specs, check_vma=False
    )
```

profile of v0, /device:TPU:0, one launch (start us, length us, event | category | flops | bytes accessed | tf_op | source)
XLA Modules:
  0.0 349.3 jit_solution(2352689093779938661)
XLA Ops:
  9.9 7.3 %all-to-all-start.4 = ((bf16[8,2,640]{2,1,0:T(2,128)(2,1)}), bf16[8,2,640]{2,1,0:T(2,128)(2,1)S(1)}, u32[]{:S(2)}, u32[]{:S(2)}) async-start(bf16[8,2,640]{2,1,0:T(2,128)(2,1)} %reshape.116), calls=%async_computation.4 | async-start | bytes 40960 | tf_op jit(solution)/shard_map/all_to_all | solution.py:73
  18.5 5.3 %all-to-all-done.4 = bf16[8,2,640]{2,1,0:T(2,128)(2,1)S(1)} async-done(((bf16[8,2,640]{2,1,0:T(2,128)(2,1)}), bf16[8,2,640]{2,1,0:T(2,128)(2,1)S(1)}, u32[]{:S(2)}, u32[]{:S(2)}) %all-to-all-start.4) | async-done | bytes 20512 | tf_op jit(solution)/shard_map/all_to_all | solution.py:73
  23.8 3.5 %all-to-all-start = ((bf16[2,256,512]{2,0,1:T(2,128)(2,1)}), bf16[2,256,512]{2,0,1:T(2,128)(2,1)S(1)}, u32[]{:S(2)}, u32[]{:S(2)}) async-start(bf16[2,256,512]{2,0,1:T(2,128)(2,1)} %copy.40), calls=%async_computation | async-start | bytes 1048576 | tf_op jit(solution)/shard_map/all_to_all | solution.py:71
  27.3 8.5 %copy.46 = bf16[2,512,2048]{2,0,1:T(2,128)(2,1)} copy(bf16[2,512,2048]{2,1,0:T(8,128)(2,1)} %param.12) | data formatting | bytes 8388608 | tf_op args[5]
  35.8 4.7 %all-to-all-done = bf16[2,256,512]{2,0,1:T(2,128)(2,1)S(1)} async-done(((bf16[2,256,512]{2,0,1:T(2,128)(2,1)}), bf16[2,256,512]{2,0,1:T(2,128)(2,1)S(1)}, u32[]{:S(2)}, u32[]{:S(2)}) %all-to-all-start) | async-done | bytes 524320 | tf_op jit(solution)/shard_map/all_to_all | solution.py:71
  40.5 4.6 %all-to-all-start.2 = ((bf16[2,512,2048]{2,0,1:T(2,128)(2,1)}), bf16[2,512,2048]{2,0,1:T(2,128)(2,1)}, u32[]{:S(2)}, u32[]{:S(2)}) async-start(bf16[2,512,2048]{2,0,1:T(2,128)(2,1)} %copy.46), calls=%async_computation.2 | async-start | bytes 8388608 | tf_op jit(solution)/shard_map/all_to_all | solution.py:72
  45.3 1.8 gather_fusion
  47.1 1.9 gather_fusion.1
  49.8 6.5 %all_gather.14 = bf16[2,2048,10]{1,2,0:T(8,128)(2,1)S(1)} all-gather(bf16[2,512,10]{1,2,0:T(8,128)(2,1)S(1)} %copy.42), channel_id=1, replica_groups=mesh['member'=8,'dp'=4] {'dp'}, dimensions={1}, use_global_device_ids=true | all-gather | bytes 102400 | tf_op jit(solution)/shard_map/all_gather | solution.py:41
  59.1 77.7 %all-to-all-done.2 = bf16[2,512,2048]{2,0,1:T(2,128)(2,1)} async-done(((bf16[2,512,2048]{2,0,1:T(2,128)(2,1)}), bf16[2,512,2048]{2,0,1:T(2,128)(2,1)}, u32[]{:S(2)}, u32[]{:S(2)}) %all-to-all-start.2) | async-done | bytes 4194336 | tf_op jit(solution)/shard_map/all_to_all | solution.py:72
  136.8 4.1 %copy.47 = bf16[2,8,64,2048]{3,2,0,1:T(8,128)(2,1)S(1)} copy(bf16[2,8,64,2048]{3,0,2,1:T(2,128)(2,1)} %bitcast.12) | data formatting | bytes 8388608 | tf_op jit(solution)/shard_map/all_to_all | solution.py:72
  140.9 4.3 %copy.56 = bf16[2,8,64,2048]{3,1,2,0:T(8,128)(2,1)} copy(bf16[2,8,64,2048]{3,2,1,0:T(8,128)(2,1)S(1)} %bitcast.93) | data formatting | bytes 8388608
  145.2 4.2 %convert_reduce_fusion = f32[64,2048]{1,0:T(8,128)S(1)} fusion(bf16[2,8,64,2048]{3,0,2,1:T(2,128)(2,1)} %bitcast.12), kind=kLoop, calls=%fused_computation.6 | loop fusion | flops 4063232 | bytes 4718592 | tf_op jit(solution)/shard_map/reduce_sum | solution.py:20
  149.6 9.9 %tanh_convert_fusion = bf16[2,256,2048]{2,1,0:T(8,128)(2,1)S(1)} fusion(bf16[2,2048,2048]{2,1,0:T(8,128)(2,1)} %all-gather.6.cloned.1.call-done, bf16[2,256,2048]{2,1,0:T(8,128)(2,1)} %all-gather.4.cloned.1.call-done, bf16[256,256]{1,0:T(8,128)(2,1)S(1)} %copy-done.5), kind=kOutput, calls=%fused_computation.7 | convolution fusion | flops 4836032512 | bytes 21102592 | tf_op jit(solution)/shard_map/jsk,jkh->jsh/dot_general | solution.py:47
  161.9 30.8 %all-gather = f32[8,2,2560]{2,1,0:T(2,128)S(1)} all-gather(f32[1,2,2560]{2,1,0:T(2,128)S(1)} %reshape.110), channel_id=1, replica_groups=mesh['member'=8,'dp'=4] {'member'}, dimensions={0}, use_global_device_ids=true | all-gather | bytes 184320 | tf_op jit(solution)/shard_map/all_gather | solution.py:57
  193.5 5.8 %all-reduce = (bf16[16,16]{1,0:T(8,128)(2,1)S(1)}, bf16[16]{0:T(256)(128)(2,1)S(1)}) all-reduce(bf16[16,16]{1,0:T(8,128)(2,1)S(1)} %convolution_convert_fusion, bf16[16]{0:T(256)(128)(2,1)S(1)} %fusion.4), channel_id=1, replica_groups=mesh['member'=8,'dp'=4] {'dp'}, use_global_device_ids=true, to_apply=%region_1.0 | all-reduce | flops 272 | bytes 1088 | tf_op jit(solution)/shard_map/psum | solution.py:63
  207.1 3.7 %all-to-all-start.5 = ((bf16[8,2,640]{2,1,0:T(2,128)(2,1)}), bf16[8,2,640]{2,1,0:T(2,128)(2,1)S(1)}, u32[]{:S(2)}, u32[]{:S(2)}) async-start(bf16[8,2,640]{2,1,0:T(2,128)(2,1)} %reshape.118), calls=%async_computation.5 | async-start | bytes 40960 | tf_op jit(solution)/shard_map/all_to_all | solution.py:83
  213.0 7.0 %fusion.29 = f32[32,131072]{1,0:T(8,128)} fusion(bf16[16,131072]{1,0:T(8,128)(2,1)S(1)} %bitcast.91, bf16[16,16]{0,1:T(8,128)(2,1)S(1)} %get-tuple-element.11, bf16[16,16]{0,1:T(8,128)(2,1)S(1)} %get-tuple-element.8), kind=kOutput, calls=%fused_computation.61 | convolution fusion | flops 134219776 | bytes 20972544 | tf_op jit(solution)/shard_map/dot_general | solution.py:17
  221.0 6.0 %all-to-all-start.1 = ((bf16[16,32,512]{2,1,0:T(8,128)(2,1)}), bf16[16,32,512]{2,1,0:T(8,128)(2,1)S(1)}, u32[]{:S(2)}, u32[]{:S(2)}) async-start(bf16[16,32,512]{2,1,0:T(8,128)(2,1)} %bitcast.30), calls=%async_computation.1 | async-start | bytes 1048576 | tf_op jit(solution)/shard_map/all_to_all | solution.py:81
  227.0 7.8 %fusion.2 = bf16[16,131072]{1,0:T(8,128)(2,1)S(1)} fusion(f32[32,131072]{1,0:T(8,128)} %fusion.29, bf16[16,131072]{1,0:T(8,128)(2,1)} %bitcast.90, f32[131072]{0:T(1024)S(1)} %bitcast.102, f32[16]{0:T(128)S(1)} %get-tuple-element.7), kind=kLoop, calls=%fused_computation.5 | loop fusion | flops 12582912 | bytes 25690176 | tf_op jit(solution)/shard_map/convert_element_type | solution.py:22
  234.8 4.3 %copy.58 = bf16[2,8,64,2048]{3,2,1,0:T(8,128)(2,1)} copy(bf16[2,8,64,2048]{3,1,2,0:T(8,128)(2,1)S(1)} %bitcast.94) | data formatting | bytes 8388608
  240.9 4.6 %all-to-all-start.3 = ((bf16[16,64,2048]{2,1,0:T(8,128)(2,1)}), bf16[16,64,2048]{2,1,0:T(8,128)(2,1)}, u32[]{:S(2)}, u32[]{:S(2)}) async-start(bf16[16,64,2048]{2,1,0:T(8,128)(2,1)} %bitcast.92), calls=%async_computation.3 | async-start | bytes 8388608 | tf_op jit(solution)/shard_map/all_to_all | solution.py:82
  247.2 90.4 %all-to-all-done.3 = bf16[16,64,2048]{2,1,0:T(8,128)(2,1)} async-done(((bf16[16,64,2048]{2,1,0:T(8,128)(2,1)}), bf16[16,64,2048]{2,1,0:T(8,128)(2,1)}, u32[]{:S(2)}, u32[]{:S(2)}) %all-to-all-start.3) | async-done | bytes 4194336 | tf_op jit(solution)/shard_map/all_to_all | solution.py:82
  337.6 4.8 %copy.48 = bf16[8,2,64,2048]{3,2,0,1:T(8,128)(2,1)} copy(bf16[8,2,64,2048]{3,2,1,0:T(8,128)(2,1)} %bitcast.14) | data formatting | bytes 8388608 | tf_op jit(solution)/shard_map/all_to_all | solution.py:82
  (83 shorter events, 25.2 us)
Async XLA Ops:
  7.2 38.1 %copy-start = (bf16[512,256]{1,0:T(8,128)(2,1)S(1)}, bf16[512,256]{1,0:T(8,128)(2,1)}, u32[]{:S(2)}) copy-start(bf16[512,256]{1,0:T(8,128)(2,1)} %param.7) | copy-start | bytes 786436
  7.2 10.0 %copy-start.4 = (bf16[2,256,512]{2,1,0:T(8,128)(2,1)S(1)}, bf16[2,256,512]{2,1,0:T(8,128)(2,1)}, u32[]{:S(2)}) copy-start(bf16[2,256,512]{2,1,0:T(8,128)(2,1)} %param.11) | copy-start | bytes 1572868
  7.2 1.5 copy-start.6
  7.2 142.4 %all-gather.4.cloned.1.call-start = ((), (), s32[]{:S(2)}) async-start(), calls=%async_computation.6 | async-start | bytes 2621440 | tf_op jit(solution)/shard_map/all_gather | solution.py:39
  7.9 141.7 %all-gather.6.cloned.1.call-start = ((), (), s32[]{:S(2)}) async-start(), calls=%async_computation.7 | async-start | bytes 20971520 | tf_op jit(solution)/shard_map/all_gather | solution.py:40
  9.9 13.9 %all-to-all-start.4 = ((bf16[8,2,640]{2,1,0:T(2,128)(2,1)}), bf16[8,2,640]{2,1,0:T(2,128)(2,1)S(1)}, u32[]{:S(2)}, u32[]{:S(2)}) async-start(bf16[8,2,640]{2,1,0:T(2,128)(2,1)} %reshape.116), calls=%async_computation.4 | async-start | bytes 40960 | tf_op jit(solution)/shard_map/all_to_all | solution.py:73
  23.8 16.8 %all-to-all-start = ((bf16[2,256,512]{2,0,1:T(2,128)(2,1)}), bf16[2,256,512]{2,0,1:T(2,128)(2,1)S(1)}, u32[]{:S(2)}, u32[]{:S(2)}) async-start(bf16[2,256,512]{2,0,1:T(2,128)(2,1)} %copy.40), calls=%async_computation | async-start | bytes 1048576 | tf_op jit(solution)/shard_map/all_to_all | solution.py:71
  35.8 9.4 %copy-start.7 = (s32[256]{0:T(256)S(1)}, s32[256]{0:T(256)}, u32[]{:S(2)}) copy-start(s32[256]{0:T(256)} %param.9) | copy-start | bytes 3076
  35.8 11.2 %copy-start.2 = (s32[512]{0:T(512)S(1)}, s32[512]{0:T(512)}, u32[]{:S(2)}) copy-start(s32[512]{0:T(512)} %param.8) | copy-start | bytes 6148
  35.8 13.2 %copy-start.9 = (f32[10]{0:T(128)S(1)}, f32[10]{0:T(128)}, u32[]{:S(2)}) copy-start(f32[10]{0:T(128)} %param.10) | copy-start | bytes 124
  40.5 96.3 %all-to-all-start.2 = ((bf16[2,512,2048]{2,0,1:T(2,128)(2,1)}), bf16[2,512,2048]{2,0,1:T(2,128)(2,1)}, u32[]{:S(2)}, u32[]{:S(2)}) async-start(bf16[2,512,2048]{2,0,1:T(2,128)(2,1)} %copy.46), calls=%async_computation.2 | async-start | bytes 8388608 | tf_op jit(solution)/shard_map/all_to_all | solution.py:72
  145.2 4.4 %copy-start.5 = (bf16[256,256]{1,0:T(8,128)(2,1)S(1)}, bf16[256,256]{1,0:T(8,128)(2,1)}, u32[]{:S(2)}) copy-start(bf16[256,256]{1,0:T(8,128)(2,1)} %gather_fusion) | copy-start | bytes 393220
  149.6 10.0 %copy-start.8 = (f32[10]{0:T(128)S(1)}, f32[10]{0:T(128)}, u32[]{:S(2)}) copy-start(f32[10]{0:T(128)} %get-tuple-element.10) | copy-start | bytes 124
  207.1 13.9 %all-to-all-start.5 = ((bf16[8,2,640]{2,1,0:T(2,128)(2,1)}), bf16[8,2,640]{2,1,0:T(2,128)(2,1)S(1)}, u32[]{:S(2)}, u32[]{:S(2)}) async-start(bf16[8,2,640]{2,1,0:T(2,128)(2,1)} %reshape.118), calls=%async_computation.5 | async-start | bytes 40960 | tf_op jit(solution)/shard_map/all_to_all | solution.py:83
  210.8 2.2 copy-start.3
  221.0 20.0 %all-to-all-start.1 = ((bf16[16,32,512]{2,1,0:T(8,128)(2,1)}), bf16[16,32,512]{2,1,0:T(8,128)(2,1)S(1)}, u32[]{:S(2)}, u32[]{:S(2)}) async-start(bf16[16,32,512]{2,1,0:T(8,128)(2,1)} %bitcast.30), calls=%async_computation.1 | async-start | bytes 1048576 | tf_op jit(solution)/shard_map/all_to_all | solution.py:81
  240.9 96.7 %all-to-all-start.3 = ((bf16[16,64,2048]{2,1,0:T(8,128)(2,1)}), bf16[16,64,2048]{2,1,0:T(8,128)(2,1)}, u32[]{:S(2)}, u32[]{:S(2)}) async-start(bf16[16,64,2048]{2,1,0:T(8,128)(2,1)} %bitcast.92), calls=%async_computation.3 | async-start | bytes 8388608 | tf_op jit(solution)/shard_map/all_to_all | solution.py:82
  337.6 4.8 %copy-start.1 = (bf16[512,256]{1,0:T(8,128)(2,1)S(1)}, bf16[512,256]{1,0:T(8,128)(2,1)}, u32[]{:S(2)}) copy-start(bf16[512,256]{1,0:T(8,128)(2,1)} %param.7) | copy-start | bytes 786436
Sparse Core Ops, SparseCore 0:
  9.6 25.2 all-gather.3
  36.5 106.5 all-gather.5
where the time goes:
time: 350 us; the launch traced here: 349 us
  waiting for transfers between devices  181 us (52%)
  blocking collectives  43.1 us (12%)
  local copies, waits for them, and re-layouts  40.9 us (12%)
  starting transfers between devices  29.8 us (9%)
  matrix products  20.6 us (6%)
  other arithmetic  19.1 us (5%)
  between operations  14.4 us (4%)
    all_to_all x1, waiting for transfers between devices, on_device(): lax.all_to_all(updated[1], 'member', split_axis=0, concat_axis=1, tiled=T...  90.4 us
    all_to_all x1, waiting for transfers between devices, on_device(): lax.all_to_all(middle_weight, 'member', split_axis=1, concat_axis=0, tile...  77.7 us
    all_gather x1, blocking collectives, on_device(): every_member = lax.all_gather(scaled, 'member', axis=0, tiled=True)  30.8 us
    unnamed x36, local copies, waits for them, and re-layouts  23.7 us
    convert_element_type x3, other arithmetic, update_piece(): return renewed.astype(jnp.bfloat16).reshape(piece.shape)  10 us
    dot_general x1, matrix products, on_device(): jnp.einsum('jsk,jkh->jsh', hidden_one, middle_full, preferred_element_typ...  9.89 us
    dot_general x3, matrix products, update_piece(): both = jnp.dot(stacked, flat, preferred_element_type=jnp.float32)  8.53 us
    all_to_all x1, starting transfers between devices, on_device(): lax.all_to_all(last_weight, 'member', split_axis=1, concat_axis=0, tiled=...  7.28 us
  transfers between devices with their start and end apart: 8, of which 5 were waited for; matrix products, arithmetic and copies ran while one was open for 15% of the time, Pallas kernels for 0%

commit v1 on v0

--- a/solution.py
+++ b/solution.py
@@ -6,6 +6,12 @@
 F_IN = 256
 H = 2048
 precise = lax.Precision.HIGHEST
+
+
+def stacked_exchange(block, axis, split, join):
+    pieces = jnp.split(block, lax.axis_size(axis), axis=split)
+    received = lax.all_to_all(jnp.stack(pieces), axis, 0, 0)
+    return jnp.concatenate(received, axis=join)
 
 
 def update_piece(piece, mixing):
@@ -79,7 +85,7 @@
     )
     new_first, new_middle, new_last = (
         lax.all_to_all(updated[0], "member", split_axis=0, concat_axis=1, tiled=True),
-        lax.all_to_all(updated[1], "member", split_axis=0, concat_axis=1, tiled=True),
+        stacked_exchange(updated[1], "member", 0, 1),
         lax.all_to_all(updated[2], "member", split_axis=0, concat_axis=1, tiled=True),
     )
     return (new_first, new_middle, new_last)

time: 350 us -> 367 us (1.049)
  local copies, waits for them, and re-layouts: 40.9 us -> 54.3 us
  waiting for transfers between devices: 181 us -> 194 us
  other arithmetic: 19.1 us -> 11.8 us
    split x0 -> x1, local copies, waits for them, and re-layouts: none -> 10.9 us  [stacked_exchange(): pieces = jnp.split(block, lax.axis_size(axis), axis=split)]
    all_to_all x1, waiting for transfers between devices: 1.8 us -> 12 us  [on_device(): lax.all_to_all(updated[0], 'member', split_axis=0, concat_axis=1, tiled=T...]
    convert_element_type x3, other arithmetic: 10 us -> 3.2 us  [update_piece(): return renewed.astype(jnp.bfloat16).reshape(piece.shape)]
    reshape x0 -> x1, local copies, waits for them, and re-layouts: none -> 4.83 us  [stacked_exchange(): return jnp.concatenate(received, axis=join)]
    all_to_all x1 -> x0, local copies, waits for them, and re-layouts: 4.83 us -> none  [on_device(): lax.all_to_all(updated[1], 'member', split_axis=0, concat_axis=1, tiled=T...]
    unnamed x36 -> x40, local copies, waits for them, and re-layouts: 23.7 us -> 27.2 us
  transfers between devices with their start and end apart: 8 -> 8, of which waited for: 5 -> 5; matrix products, arithmetic and copies ran while one was open for 15% -> 11% of each run, Pallas kernels for 0% -> 0%
where the time goes in v1:
time: 367 us
  waiting for transfers between devices  194 us (53%)
  local copies, waits for them, and re-layouts  54.3 us (15%)
  blocking collectives  43.1 us (12%)
  starting transfers between devices  29.8 us (8%)
  matrix products  19.3 us (5%)
  between operations  14.4 us (4%)
  other arithmetic  11.8 us (3%)
    all_to_all x1, waiting for transfers between devices, stacked_exchange(): received = lax.all_to_all(jnp.stack(pieces), axis, 0, 0)  90.4 us
    all_to_all x1, waiting for transfers between devices, on_device(): lax.all_to_all(middle_weight, 'member', split_axis=1, concat_axis=0, tile...  80.1 us
    all_gather x1, blocking collectives, on_device(): every_member = lax.all_gather(scaled, 'member', axis=0, tiled=True)  30.8 us
    unnamed x40, local copies, waits for them, and re-layouts  27.2 us
    all_to_all x1, waiting for transfers between devices, on_device(): lax.all_to_all(updated[0], 'member', split_axis=0, concat_axis=1, tiled=T...  12 us
    dot_general x1, matrix products, on_device(): jnp.einsum('jsk,jkh->jsh', hidden_one, middle_full, preferred_element_typ...  10.9 us
    split x1, local copies, waits for them, and re-layouts, stacked_exchange(): pieces = jnp.split(block, lax.axis_size(axis), axis=split)  10.9 us
  transfers between devices with their start and end apart: 8, of which 5 were waited for; matrix products, arithmetic and copies ran while one was open for 11% of the time, Pallas kernels for 0%

profile of v1, /device:TPU:0, one launch (start us, length us, event | category | flops | bytes accessed | tf_op | source)
XLA Modules:
  0.0 366.6 jit_solution(1965884118945550099)
XLA Ops:
  9.9 7.3 %all-to-all-start.4 = ((bf16[8,2,640]{2,1,0:T(2,128)(2,1)}), bf16[8,2,640]{2,1,0:T(2,128)(2,1)S(1)}, u32[]{:S(2)}, u32[]{:S(2)}) async-start(bf16[8,2,640]{2,1,0:T(2,128)(2,1)} %reshape.137), calls=%async_computation.4 | async-start | bytes 40960 | tf_op jit(solution)/shard_map/all_to_all | solution.py:79
  18.5 5.3 %all-to-all-done.4 = bf16[8,2,640]{2,1,0:T(2,128)(2,1)S(1)} async-done(((bf16[8,2,640]{2,1,0:T(2,128)(2,1)}), bf16[8,2,640]{2,1,0:T(2,128)(2,1)S(1)}, u32[]{:S(2)}, u32[]{:S(2)}) %all-to-all-start.4) | async-done | bytes 20512 | tf_op jit(solution)/shard_map/all_to_all | solution.py:79
  23.8 3.5 all-to-all-start
  27.3 8.5 %copy.46 = bf16[2,512,2048]{2,0,1:T(2,128)(2,1)} copy(bf16[2,512,2048]{2,1,0:T(8,128)(2,1)} %param.12) | data formatting | bytes 8388608 | tf_op args[5]
  35.8 4.7 %all-to-all-done = bf16[2,256,512]{2,0,1:T(2,128)(2,1)S(1)} async-done(((bf16[2,256,512]{2,0,1:T(2,128)(2,1)}), bf16[2,256,512]{2,0,1:T(2,128)(2,1)S(1)}, u32[]{:S(2)}, u32[]{:S(2)}) %all-to-all-start) | async-done | bytes 524320 | tf_op jit(solution)/shard_map/all_to_all | solution.py:77
  40.5 4.6 %all-to-all-start.2 = ((bf16[2,512,2048]{2,0,1:T(2,128)(2,1)}), bf16[2,512,2048]{2,0,1:T(2,128)(2,1)}, u32[]{:S(2)}, u32[]{:S(2)}) async-start(bf16[2,512,2048]{2,0,1:T(2,128)(2,1)} %copy.46), calls=%async_computation.2 | async-start | bytes 8388608 | tf_op jit(solution)/shard_map/all_to_all | solution.py:78
  48.6 6.5 %all_gather.14 = bf16[2,2048,10]{1,2,0:T(8,128)(2,1)S(1)} all-gather(bf16[2,512,10]{1,2,0:T(8,128)(2,1)S(1)} %copy.42), channel_id=1, replica_groups=mesh['member'=8,'dp'=4] {'dp'}, dimensions={1}, use_global_device_ids=true | all-gather | bytes 102400 | tf_op jit(solution)/shard_map/all_gather | solution.py:47
  56.7 80.1 %all-to-all-done.2 = bf16[2,512,2048]{2,0,1:T(2,128)(2,1)} async-done(((bf16[2,512,2048]{2,0,1:T(2,128)(2,1)}), bf16[2,512,2048]{2,0,1:T(2,128)(2,1)}, u32[]{:S(2)}, u32[]{:S(2)}) %all-to-all-start.2) | async-done | bytes 4194336 | tf_op jit(solution)/shard_map/all_to_all | solution.py:78
  136.8 4.1 %copy.47 = bf16[2,8,64,2048]{3,2,0,1:T(8,128)(2,1)S(1)} copy(bf16[2,8,64,2048]{3,0,2,1:T(2,128)(2,1)} %bitcast.12) | data formatting | bytes 8388608 | tf_op jit(solution)/shard_map/all_to_all | solution.py:78
  140.9 4.3 %copy.56 = bf16[2,8,64,2048]{3,1,2,0:T(8,128)(2,1)} copy(bf16[2,8,64,2048]{3,2,1,0:T(8,128)(2,1)S(1)} %bitcast.120) | data formatting | bytes 8388608
  145.2 4.2 %convert_reduce_fusion = f32[64,2048]{1,0:T(8,128)S(1)} fusion(bf16[2,8,64,2048]{3,0,2,1:T(2,128)(2,1)} %bitcast.12), kind=kLoop, calls=%fused_computation.6 | loop fusion | flops 4063232 | bytes 4718592 | tf_op jit(solution)/shard_map/reduce_sum | solution.py:26
  149.6 10.9 %tanh_convert_fusion = bf16[2,256,2048]{2,1,0:T(8,128)(2,1)} fusion(bf16[2,2048,2048]{2,1,0:T(8,128)(2,1)} %all-gather.6.cloned.1.call-done, bf16[2,256,2048]{2,1,0:T(8,128)(2,1)} %all-gather.4.cloned.1.call-done, bf16[256,256]{1,0:T(8,128)(2,1)S(1)} %gather_fusion), kind=kOutput, calls=%fused_computation.7 | convolution fusion | flops 4836032512 | bytes 21102592 | tf_op jit(solution)/shard_map/jsk,jkh->jsh/dot_general | solution.py:53
  160.5 2.2 convolution_multiply_fusion
  163.1 30.8 %all-gather = f32[8,2,2560]{2,1,0:T(2,128)S(1)} all-gather(f32[1,2,2560]{2,1,0:T(2,128)S(1)} %reshape.131), channel_id=1, replica_groups=mesh['member'=8,'dp'=4] {'member'}, dimensions={0}, use_global_device_ids=true | all-gather | bytes 184320 | tf_op jit(solution)/shard_map/all_gather | solution.py:63
  194.7 5.8 %all-reduce = (bf16[16,16]{1,0:T(8,128)(2,1)S(1)}, bf16[16]{0:T(256)(128)(2,1)S(1)}) all-reduce(bf16[16,16]{1,0:T(8,128)(2,1)S(1)} %convolution_convert_fusion, bf16[16]{0:T(256)(128)(2,1)S(1)} %fusion.4), channel_id=1, replica_groups=mesh['member'=8,'dp'=4] {'dp'}, use_global_device_ids=true, to_apply=%region_1.0 | all-reduce | flops 272 | bytes 1088 | tf_op jit(solution)/shard_map/psum | solution.py:69
  205.0 4.5 %fusion.29 = f32[32,131072]{1,0:T(8,128)S(1)} fusion(bf16[16,131072]{1,0:T(8,128)(2,1)} %bitcast.118, bf16[16,16]{0,1:T(8,128)(2,1)S(1)} %get-tuple-element.19, bf16[16,16]{0,1:T(8,128)(2,1)S(1)} %get-tuple-element.16), kind=kOutput, calls=%fused_computation.69 | convolution fusion | flops 134219776 | bytes 20972544 | tf_op jit(solution)/shard_map/dot_general | solution.py:23
  209.5 2.9 fusion.2
  212.4 10.9 %fusion.31 = (bf16[2,131072]{1,0:T(2,128)(2,1)S(1)}, bf16[2,131072]{1,0:T(2,128)(2,1)S(1)}, bf16[2,131072]{1,0:T(2,128)(2,1)S(1)}, bf16[2,131072]{1,0:T(2,128)(2...) fusion(bf16[16,131072]{1,0:T(8,128)(2,1)} %fusion.2), kind=kLoop, calls=%fused_computation.71 | loop fusion | bytes 8388608 | tf_op jit(solution)/shard_map/split | solution.py:12
  226.0 3.7 %all-to-all-start.5 = ((bf16[8,2,640]{2,1,0:T(2,128)(2,1)}), bf16[8,2,640]{2,1,0:T(2,128)(2,1)S(1)}, u32[]{:S(2)}, u32[]{:S(2)}) async-start(bf16[8,2,640]{2,1,0:T(2,128)(2,1)} %reshape.139), calls=%async_computation.5 | async-start | bytes 40960 | tf_op jit(solution)/shard_map/all_to_all | solution.py:89
  238.3 6.0 %all-to-all-start.1 = ((bf16[16,32,512]{2,1,0:T(8,128)(2,1)}), bf16[16,32,512]{2,1,0:T(8,128)(2,1)S(1)}, u32[]{:S(2)}, u32[]{:S(2)}) async-start(bf16[16,32,512]{2,1,0:T(8,128)(2,1)} %bitcast.28), calls=%async_computation.1 | async-start | bytes 1048576 | tf_op jit(solution)/shard_map/all_to_all | solution.py:87
  246.2 12.0 %all-to-all-done.1 = bf16[16,32,512]{2,1,0:T(8,128)(2,1)S(1)} async-done(((bf16[16,32,512]{2,1,0:T(8,128)(2,1)}), bf16[16,32,512]{2,1,0:T(8,128)(2,1)S(1)}, u32[]{:S(2)}, u32[]{:S(2)}) %all-to-all-start.1) | async-done | bytes 524320 | tf_op jit(solution)/shard_map/all_to_all | solution.py:87
  258.2 4.6 %all-to-all-start.3 = ((bf16[8,2,64,2048]{3,2,1,0:T(8,128)(2,1)}), bf16[8,2,64,2048]{3,2,1,0:T(8,128)(2,1)}, u32[]{:S(2)}, u32[]{:S(2)}) async-start(bf16[8,2,64,2048]{3,2,1,0:T(8,128)(2,1)} %bitcast_dynamic-update-slice_fusion), calls=%async_computation.3 | async-start | bytes 8388608 | tf_op jit(solution)/shard_map/all_to_all | solution.py:13
  264.5 90.4 %all-to-all-done.3 = bf16[8,2,64,2048]{3,2,1,0:T(8,128)(2,1)} async-done(((bf16[8,2,64,2048]{3,2,1,0:T(8,128)(2,1)}), bf16[8,2,64,2048]{3,2,1,0:T(8,128)(2,1)}, u32[]{:S(2)}, u32[]{:S(2)}) %all-to-all-start.3) | async-done | bytes 4194336 | tf_op jit(solution)/shard_map/all_to_all | solution.py:13
  354.9 4.8 %copy.48 = bf16[2,8,64,2048]{3,2,1,0:T(8,128)(2,1)} copy(bf16[2,8,64,2048]{3,2,0,1:T(8,128)(2,1)} %bitcast.14) | data formatting | bytes 8388608 | tf_op jit(solution)/shard_map/reshape | solution.py:14
  (89 shorter events, 29.5 us)
Async XLA Ops:
  7.2 38.1 %copy-start = (bf16[512,256]{1,0:T(8,128)(2,1)S(1)}, bf16[512,256]{1,0:T(8,128)(2,1)}, u32[]{:S(2)}) copy-start(bf16[512,256]{1,0:T(8,128)(2,1)} %param.7) | copy-start | bytes 786436
  7.2 10.0 %copy-start.5 = (bf16[2,256,512]{2,1,0:T(8,128)(2,1)S(1)}, bf16[2,256,512]{2,1,0:T(8,128)(2,1)}, u32[]{:S(2)}) copy-start(bf16[2,256,512]{2,1,0:T(8,128)(2,1)} %param.11) | copy-start | bytes 1572868
  7.2 1.5 copy-start.6
  7.2 142.4 %all-gather.4.cloned.1.call-start = ((), (), s32[]{:S(2)}) async-start(), calls=%async_computation.6 | async-start | bytes 2621440 | tf_op jit(solution)/shard_map/all_gather | solution.py:45
  7.9 141.6 %all-gather.6.cloned.1.call-start = ((), (), s32[]{:S(2)}) async-start(), calls=%async_computation.7 | async-start | bytes 20971520 | tf_op jit(solution)/shard_map/all_gather | solution.py:46
  9.9 13.9 %all-to-all-start.4 = ((bf16[8,2,640]{2,1,0:T(2,128)(2,1)}), bf16[8,2,640]{2,1,0:T(2,128)(2,1)S(1)}, u32[]{:S(2)}, u32[]{:S(2)}) async-start(bf16[8,2,640]{2,1,0:T(2,128)(2,1)} %reshape.137), calls=%async_computation.4 | async-start | bytes 40960 | tf_op jit(solution)/shard_map/all_to_all | solution.py:79
  23.8 16.8 %all-to-all-start = ((bf16[2,256,512]{2,0,1:T(2,128)(2,1)}), bf16[2,256,512]{2,0,1:T(2,128)(2,1)S(1)}, u32[]{:S(2)}, u32[]{:S(2)}) async-start(bf16[2,256,512]{2,0,1:T(2,128)(2,1)} %copy.40), calls=%async_computation | async-start | bytes 1048576 | tf_op jit(solution)/shard_map/all_to_all | solution.py:77
  35.8 9.4 %copy-start.7 = (s32[256]{0:T(256)S(1)}, s32[256]{0:T(256)}, u32[]{:S(2)}) copy-start(s32[256]{0:T(256)} %param.9) | copy-start | bytes 3076
  35.8 10.6 %copy-start.2 = (s32[512]{0:T(512)S(1)}, s32[512]{0:T(512)}, u32[]{:S(2)}) copy-start(s32[512]{0:T(512)} %param.8) | copy-start | bytes 6148
  35.8 12.5 %copy-start.8 = (f32[10]{0:T(128)S(1)}, f32[10]{0:T(128)}, u32[]{:S(2)}) copy-start(f32[10]{0:T(128)} %param.10) | copy-start | bytes 124
  40.5 96.3 %all-to-all-start.2 = ((bf16[2,512,2048]{2,0,1:T(2,128)(2,1)}), bf16[2,512,2048]{2,0,1:T(2,128)(2,1)}, u32[]{:S(2)}, u32[]{:S(2)}) async-start(bf16[2,512,2048]{2,0,1:T(2,128)(2,1)} %copy.46), calls=%async_computation.2 | async-start | bytes 8388608 | tf_op jit(solution)/shard_map/all_to_all | solution.py:78
  205.0 4.5 %copy-start.3 = (bf16[2,8,64,2048]{3,1,2,0:T(8,128)(2,1)S(1)}, bf16[2,8,64,2048]{3,1,2,0:T(8,128)(2,1)}, u32[]{:S(2)}) copy-start(bf16[2,8,64,2048]{3,1,2,0:T(8,128)(2,1)} %copy.56) | copy-start | bytes 12582916
  226.0 12.3 %all-to-all-start.5 = ((bf16[8,2,640]{2,1,0:T(2,128)(2,1)}), bf16[8,2,640]{2,1,0:T(2,128)(2,1)S(1)}, u32[]{:S(2)}, u32[]{:S(2)}) async-start(bf16[8,2,640]{2,1,0:T(2,128)(2,1)} %reshape.139), calls=%async_computation.5 | async-start | bytes 40960 | tf_op jit(solution)/shard_map/all_to_all | solution.py:89
  229.7 4.5 %copy-start.4 = (bf16[2,131072]{1,0:T(2,128)(2,1)S(1)}, bf16[2,131072]{1,0:T(2,128)(2,1)}, u32[]{:S(2)}) copy-start(bf16[2,131072]{1,0:T(2,128)(2,1)} %get-tuple-element.9) | copy-start | bytes 1572868
  238.3 19.9 %all-to-all-start.1 = ((bf16[16,32,512]{2,1,0:T(8,128)(2,1)}), bf16[16,32,512]{2,1,0:T(8,128)(2,1)S(1)}, u32[]{:S(2)}, u32[]{:S(2)}) async-start(bf16[16,32,512]{2,1,0:T(8,128)(2,1)} %bitcast.28), calls=%async_computation.1 | async-start | bytes 1048576 | tf_op jit(solution)/shard_map/all_to_all | solution.py:87
  258.2 96.7 %all-to-all-start.3 = ((bf16[8,2,64,2048]{3,2,1,0:T(8,128)(2,1)}), bf16[8,2,64,2048]{3,2,1,0:T(8,128)(2,1)}, u32[]{:S(2)}, u32[]{:S(2)}) async-start(bf16[8,2,64,2048]{3,2,1,0:T(8,128)(2,1)} %bitcast_dynamic-update-slice_fusion), calls=%async_computation.3 | async-start | bytes 8388608 | tf_op jit(solution)/shard_map/all_to_all | solution.py:13
  354.9 4.8 %copy-start.1 = (bf16[512,256]{1,0:T(8,128)(2,1)S(1)}, bf16[512,256]{1,0:T(8,128)(2,1)}, u32[]{:S(2)}) copy-start(bf16[512,256]{1,0:T(8,128)(2,1)} %param.7) | copy-start | bytes 786436
Sparse Core Ops, SparseCore 0:
  9.6 25.2 all-gather.3
  36.5 106.5 all-gather.5
